TPU v7x, 32 devices: a whole 2x2x4 slice. The times are simulated.
32 devices in a mesh: dp: 4 (over x, core), fsdp: 8 (over z, y).
Axes of the slice: x: 2, y: 2, z: 4, core: 2. Of those that a mesh axis runs over, the one named last changes fastest.
Arguments:
- tokens: bfloat16 [4, 1024, 768], P('dp', 'fsdp'), may hold values from -6 to 6
- ln1_gain: bfloat16 [768], P('fsdp'), may hold values from 0.099609375 to 1.8984375
- ln1_bias: bfloat16 [768], P('fsdp'), may hold values from -1.75 to 1.75
- ln2_gain: bfloat16 [768], P('fsdp'), may hold values from 0.099609375 to 1.8984375
- ln2_bias: bfloat16 [768], P('fsdp'), may hold values from -1.75 to 1.75
- qkv_weight: bfloat16 [768, 2304], P('fsdp'), may hold values from -0.21875 to 0.21875
- qkv_bias: bfloat16 [2304], P('fsdp'), may hold values from -3 to 3
- out_weight: bfloat16 [768, 768], P('fsdp'), may hold values from -1.75 to 1.75
- out_bias: bfloat16 [768], P('fsdp'), may hold values from -3 to 3
- up_weight: bfloat16 [768, 3072], P('fsdp'), may hold values from -0.21875 to 0.21875
- up_bias: bfloat16 [3072], P('fsdp'), may hold values from -3 to 3
- down_weight: bfloat16 [3072, 768], P('fsdp'), may hold values from -0.109375 to 0.109375
- down_bias: bfloat16 [768], P('fsdp'), may hold values from -3 to 3
- cotangent: bfloat16 [4, 1024, 768], P('dp', 'fsdp'), may hold values from -6 to 6
Outputs:
- layer_output: bfloat16 [4, 1024, 768], P('dp', 'fsdp')
- input_grad: float32 [4, 1024, 768], P('dp', 'fsdp')
- grad_ln1_gain: float32 [768], P('fsdp')
- grad_ln1_bias: float32 [768], P('fsdp')
- grad_ln2_gain: float32 [768], P('fsdp')
- grad_ln2_bias: float32 [768], P('fsdp')
- grad_qkv_weight: float32 [768, 2304], P('fsdp')
- grad_qkv_bias: float32 [2304], P('fsdp')
- grad_out_weight: float32 [768, 768], P('fsdp')
- grad_out_bias: float32 [768], P('fsdp')
- grad_up_weight: float32 [768, 3072], P('fsdp')
- grad_up_bias: float32 [3072], P('fsdp')
- grad_down_weight: float32 [3072, 768], P('fsdp')
- grad_down_bias: float32 [768], P('fsdp')
All inputs are finite; a program needn't handle non-finite values.
Results may differ from a plain program's by a relative error of at most 0.018.
Values may be sent and summed in bfloat16 or wider, within the bound.
A program may use at most 128 MiB of HBM per device.

v0:
```python
import math
import jax
import jax.numpy as jnp
from jax import lax
from jax.sharding import PartitionSpec as P

HEADS = 12
HEAD = 64
ROT = 16
epsilon = 1e-05
inv_root_two = 1.0 / math.sqrt(2.0)
inv_root_twopi = 1.0 / math.sqrt(2.0 * math.pi)
bf16 = jnp.bfloat16
f32 = jnp.float32


def rotary(tensor, cosine, sine, direction):
    half = ROT // 2
    first = tensor[..., :half]
    second = tensor[..., half:ROT]
    return jnp.concatenate(
        [
            first * cosine - direction * second * sine,
            second * cosine + direction * first * sine,
            tensor[..., ROT:],
        ],
        axis=-1,
    )


def dot(a, b, dims):
    return lax.dot_general(a, b, ((dims[0], dims[1]), ((), ())), preferred_element_type=f32)


NN = ((1,), (0,))
NT = ((1,), (1,))
TN = ((0,), (0,))


def gather_rows(arrays):
    return [lax.all_gather(a, "fsdp", axis=0, tiled=True) for a in arrays]


def scatter_rows(a):
    return lax.psum_scatter(a, "fsdp", scatter_dimension=0, tiled=True)


def spread_weights(blocks):
    return lax.all_to_all(blocks, "fsdp", 0, 0, tiled=True)


def return_grads(blocks, own):
    summed = lax.psum(blocks, "dp")
    own = lax.psum(own, "dp")
    return (lax.all_to_all(summed, "fsdp", 0, 0, tiled=True), own)


def body(
    tokens,
    ln1_gain,
    ln1_bias,
    ln2_gain,
    ln2_bias,
    qkv_weight,
    qkv_bias,
    out_weight,
    out_bias,
    up_weight,
    up_bias,
    down_weight,
    down_bias,
    cotangent,
):
    rank = lax.axis_index("fsdp")
    F = lax.axis_size("fsdp")
    rows, D = tokens.shape[1:]
    W = D // F
    FFW = down_weight.shape[0]
    NH = max((-(-(g * W % HEAD + W) // HEAD) for g in range(F)))
    WIN = NH * HEAD
    starts = [min(g * W // HEAD, HEADS - NH) * HEAD for g in range(F)]
    start = jnp.minimum(rank * W // HEAD, HEADS - NH) * HEAD
    off = rank * W - start
    S = rows * F
    qkv3 = qkv_weight.reshape(W, 3, D)
    blocks = jnp.stack(
        [
            jnp.concatenate(
                [
                    qkv3[:, 0, s : s + WIN],
                    qkv3[:, 1, s : s + WIN],
                    qkv3[:, 2, s : s + WIN],
                    up_weight[:, g * FFW : (g + 1) * FFW],
                ],
                axis=1,
            )
            for g, s in enumerate(starts)
        ]
    )
    smalls = jnp.concatenate(
        [ln1_gain, ln1_bias, ln2_gain, ln2_bias, out_bias, down_bias, qkv_bias]
    )[None]
    x_low, small_all = gather_rows([tokens[0], smalls])
    wall = spread_weights(blocks).reshape(D, 3 * WIN + FFW)
    w_qkv = wall[:, : 3 * WIN]
    w_up = wall[:, 3 * WIN :]
    up_ring = [(i, (i + 1) % F) for i in range(F)]
    down_ring = [(i, (i - 1) % F) for i in range(F)]
    out_prev = lax.ppermute(out_weight, "fsdp", up_ring)
    out_next = lax.ppermute(out_weight, "fsdp", down_ring)
    (grad_out,) = gather_rows([cotangent[0]])
    out_three = jnp.concatenate([out_prev, out_weight, out_next, jnp.zeros((WIN, D), bf16)], axis=0)
    w_out_win = lax.dynamic_slice_in_dim(out_three, W - off, WIN, 0)
    win_col = jnp.arange(WIN, dtype=jnp.int32)
    mine = (win_col >= off) & (win_col < off + W)
    small_all = small_all.astype(f32)
    gain_one, bias_one, gain_two, bias_two, b_out, b_down = [
        small_all[:, i * W : (i + 1) * W].reshape(D) for i in range(6)
    ]
    b_qkv = small_all[:, 6 * W :].reshape(3, D)
    b_qkv = lax.dynamic_slice_in_dim(b_qkv, start, WIN, 1).reshape(3 * WIN)
    b_up = up_bias.astype(f32)
    x = x_low.astype(f32)
    center = x - jnp.mean(x, axis=-1, keepdims=True)
    inverse = lax.rsqrt(jnp.mean(center * center, axis=-1, keepdims=True) + epsilon)
    normed = center * inverse
    first_low = (normed * gain_one + bias_one).astype(bf16)
    second_low = (normed * gain_two + bias_two).astype(bf16)
    places = jnp.arange(S, dtype=f32)
    half = ROT // 2
    freq = 10000.0 ** (-(jnp.arange(half, dtype=f32) * 2.0) / ROT)
    angle = places[:, None] * freq[None, :]
    cosine = jnp.cos(angle)[:, None, :]
    sine = jnp.sin(angle)[:, None, :]
    proj = dot(first_low, w_qkv, NN) + b_qkv
    queries = (rotary(proj[:, :WIN].reshape(S, NH, HEAD), cosine, sine, 1.0) * 0.125).astype(bf16)
    keys = rotary(proj[:, WIN : 2 * WIN].reshape(S, NH, HEAD), cosine, sine, 1.0).astype(bf16)
    vals = proj[:, 2 * WIN :].astype(bf16).reshape(S, NH, HEAD)
    q_place = jnp.arange(S, dtype=jnp.int32)
    visible = (q_place[None, :] <= q_place[:, None])[None]
    scores = jnp.einsum("qhd,khd->hqk", queries, keys, preferred_element_type=f32)
    masked = jnp.where(visible, scores, -1e30)
    top = jnp.max(masked, axis=-1, keepdims=True)
    lse = top + jnp.log(jnp.sum(jnp.exp(masked - top), axis=-1, keepdims=True))
    probs = jnp.exp(masked - lse)
    probs_low = probs.astype(bf16)
    attended = jnp.einsum("hqk,khd->qhd", probs_low, vals, preferred_element_type=f32)
    att_low = jnp.where(mine, attended.reshape(S, WIN), 0.0).astype(bf16)
    hidden_pre = dot(second_low, w_up, NN) + b_up
    cdf = 0.5 * (1.0 + lax.erf(hidden_pre * inv_root_two))
    hidden_low = (hidden_pre * cdf).astype(bf16)
    part = dot(att_low, w_out_win, NN) + dot(hidden_low, down_weight, NN)
    branch = scatter_rows(part.astype(bf16)).astype(f32)
    grad_hidden = dot(grad_out, down_weight, NT)
    slope = cdf + hidden_pre * jnp.exp(-0.5 * hidden_pre * hidden_pre) * inv_root_twopi
    grad_pre = (grad_hidden * slope).astype(bf16)
    grad_w_down = dot(hidden_low, grad_out, TN)
    grad_w_out_win = dot(att_low, grad_out, TN)
    grad_w_out = lax.dynamic_slice_in_dim(grad_w_out_win, off, W, 0)
    bias_total = jnp.sum(grad_out.astype(f32), axis=0)
    grad_b_up = jnp.sum(grad_pre.astype(f32), axis=0)
    grad_att = dot(grad_out, w_out_win, NT).astype(bf16).reshape(S, NH, HEAD)
    delta = jnp.transpose(jnp.sum(grad_att.astype(f32) * attended, axis=-1))[:, :, None]
    grad_probs = jnp.einsum("qhd,khd->hqk", grad_att, vals, preferred_element_type=f32)
    grad_scores = (probs * (grad_probs - delta)).astype(bf16)
    grad_q = jnp.einsum("hqk,khd->qhd", grad_scores, keys, preferred_element_type=f32)
    grad_k = jnp.einsum("hqk,qhd->khd", grad_scores, queries, preferred_element_type=f32)
    grad_v = jnp.einsum("hqk,qhd->khd", probs_low, grad_att, preferred_element_type=f32)
    grad_proj = jnp.stack(
        [
            rotary(grad_q * 0.125, cosine, sine, -1.0).reshape(S, WIN),
            rotary(grad_k, cosine, sine, -1.0).reshape(S, WIN),
            grad_v.reshape(S, WIN),
        ],
        axis=1,
    )
    grad_proj = jnp.where(mine, grad_proj, 0.0).astype(bf16).reshape(S, 3 * WIN)
    grad_w_qkv = dot(first_low, grad_proj, TN)
    grad_w_up = dot(second_low, grad_pre, TN)
    grad_b_qkv = jnp.sum(grad_proj.astype(f32), axis=0).reshape(3, WIN)
    grad_first = dot(grad_proj, w_qkv, NT)
    grad_second = dot(grad_pre, w_up, NT)
    vectors = [
        jnp.sum(grad_first * normed, axis=0),
        jnp.sum(grad_first, axis=0),
        jnp.sum(grad_second * normed, axis=0),
        jnp.sum(grad_second, axis=0),
    ]
    mixed = grad_first * gain_one + grad_second * gain_two
    b_full = lax.dynamic_update_slice_in_dim(jnp.zeros((3, D), f32), grad_b_qkv, start, 1)
    small_part = jnp.concatenate(
        [v.reshape(F, W) for v in vectors] + [b_full.reshape(F, 3 * W)], axis=1
    )
    mixed_mine = scatter_rows(mixed.astype(bf16)).astype(f32)
    small_mine = scatter_rows(small_part)[0]
    own_small = jnp.concatenate(
        [small_mine, lax.dynamic_slice_in_dim(bias_total, rank * W, W, 0), grad_b_up]
    )
    own_small = lax.psum(own_small, "dp")
    grad_blocks = jnp.concatenate([grad_w_qkv, grad_w_up], axis=1).astype(bf16)
    grad_blocks = grad_blocks.reshape(F, W, 3 * WIN + FFW)
    own = jnp.concatenate([grad_w_out, grad_w_down], axis=0).astype(bf16)
    returned, own = return_grads(grad_blocks, own)
    returned = returned.astype(f32)
    own = own.astype(f32)
    pieces = [
        [
            returned[g, :, i * WIN + g * W - s : i * WIN + g * W - s + W]
            for g, s in enumerate(starts)
        ]
        for i in range(3)
    ]
    out_w_qkv = jnp.concatenate(pieces[0] + pieces[1] + pieces[2], axis=1)
    out_w_up = jnp.concatenate([returned[g, :, 3 * WIN :] for g in range(F)], axis=1)
    here = rank * rows
    x_own = tokens[0].astype(f32)
    c_own = x_own - jnp.mean(x_own, axis=-1, keepdims=True)
    i_own = lax.rsqrt(jnp.mean(c_own * c_own, axis=-1, keepdims=True) + epsilon)
    n_own = c_own * i_own
    layer_output = (x_own + branch + b_out + b_down).astype(bf16)
    input_grad = cotangent[0].astype(f32) + i_own * (
        mixed_mine
        - jnp.mean(mixed_mine, axis=-1, keepdims=True)
        - n_own * jnp.mean(mixed_mine * n_own, axis=-1, keepdims=True)
    )
    g = [own_small[i * W : (i + 1) * W] for i in range(4)]
    bias_mine = own_small[7 * W : 8 * W]
    return (
        layer_output[None],
        input_grad[None],
        g[0],
        g[1],
        g[2],
        g[3],
        out_w_qkv,
        own_small[4 * W : 7 * W],
        own[:W],
        bias_mine,
        out_w_up,
        own_small[8 * W :],
        own[W:],
        bias_mine,
    )


def solution(mesh):
    row = P("fsdp", None)
    vec = P("fsdp")
    act = P("dp", "fsdp", None)
    return jax.shard_map(
        body,
        mesh=mesh,
        in_specs=(act, vec, vec, vec, vec, row, vec, row, vec, row, vec, row, vec, act),
        out_specs=(act, act, vec, vec, vec, vec, row, vec, row, vec, row, vec, row, vec),
        check_vma=False,
    )
```

profile of v0, /device:TPU:0, one launch (start us, length us, event | category | flops | bytes accessed | tf_op | source)
XLA Modules:
  0.0 361.6 jit_solution(6648687961368923165)
XLA Ops:
  7.2 3.0 collective-permute-start
  10.3 3.1 collective-permute-start.1
  13.4 1.6 reshape.208
  22.3 4.2 %all-to-all-start = ((bf16[8,96,768]{2,1,0:T(8,128)(2,1)}), bf16[8,96,768]{2,1,0:T(8,128)(2,1)}, u32[]{:S(2)}, u32[]{:S(2)}) async-start(bf16[8,96,768]{2,1,0:T(8,128)(2,1)} %fusion.81), calls=%async_computation | async-start | bytes 2359296 | tf_op jit(solution)/shard_map/all_to_all | solution.py:49
  29.0 64.6 %all-reduce = bf16[6912]{0:T(1024)(128)(2,1)S(1)} all-reduce(bf16[6912]{0:T(1024)(128)(2,1)S(1)} %dynamic-update-slice), channel_id=3, replica_groups=mesh['dp'=4,'fsdp'=8] {'fsdp'}, use_global_device_ids=true, to_apply=%add | all-reduce | flops 6912 | bytes 27648
  97.8 1.8 convert_reduce_fusion
  100.4 2.2 convolution_add_fusion.1
  104.2 1.7 select_reduce_fusion
  105.9 1.7 exponential_reduce_fusion
  107.7 1.5 copy-done.4
  109.8 6.8 %all-gather.8.cloned.1.call-done = bf16[1,1024,768]{2,1,0:T(8,128)(2,1)} async-done(((bf16[1,128,768]{2,1,0:T(8,128)(2,1)}), bf16[1,1024,768]{2,1,0:T(8,128)(2,1)}) %all-gather.8.cloned.1.call-update) | async-done | bytes 1572880 | tf_op jit(solution)/shard_map/all_gather | solution.py:41
  116.6 2.2 fusion.36
  118.9 6.5 %fusion.41 = (f32[1024,2]{0,1:T(2,128)S(1)}, bf16[2,64,1024]{2,1,0:T(8,128)(2,1)}) fusion(bf16[128,1024]{1,0:T(8,128)(2,1)S(1)} %fusion.36, bf16[1024,2,64]{0,2,1:T(8,128)(2,1)S(1)} %bitcast.330, f32[2,1024,1024]{1,2,0:T(8,128)} %copy-done.4, f32[2,1024]{1,0:T(2,128)S(1)} %copy-done.23, pred[1024,1024]{0,1:T(8,128)(4,1)S(1)} %iota_compare_fusion), kind=kOutput, calls=%fused_computation.73 | convolution fusion | flops 275249152 | bytes 10240000 | tf_op jit(solution)/shard_map/hqk,khd->qhd/dot_general | solution.py:147
  125.3 3.3 multiply_convert_fusion
  129.6 1.4 convolution_bitcast_fusion
  131.0 2.4 fusion.83
  136.0 2.3 multiply_convert_fusion.1
  138.3 1.4 convert_reduce_fusion.2
  139.6 2.1 fusion.42
  141.7 1.8 convolution_convert_fusion
  144.2 4.6 %fusion.99 = (f32[768]{0:T(1024)S(1)}, f32[768]{0:T(1024)S(1)}, bf16[1024,768]{1,0:T(8,128)(2,1)}, f32[768]{0:T(1024)S(1)}, f32[768]{0:T(1024)S(1)}, /*index=5*/bf16[768,1024]{0,1:T(8,128)(2,1)}) fusion(f32[1024,768]{1,0:T(8,128)S(1)} %fusion.42, f32[1024]{0:T(1024)S(1)} %add_rsqrt_fusion, f32[1024]{0:T(1024)S(1)} %broadcast_multiply_fusion.1, ...), kind=kOutput, calls=%fused_computation.216 | convolution fusion | flops 616559616 | bytes 9270272 | tf_op jit(solution)/shard_map/dot_general | solution.py:32
  148.9 1.7 copy.54
  151.7 2.2 convolution_convert_fusion.1
  158.5 46.5 %all-reduce.5.cloned.1.call-done = (bf16[8,96,768]{2,1,0:T(8,128)(2,1)}, bf16[480,768]{1,0:T(8,128)(2,1)}) async-done(((bf16[8,96,768]{2,1,0:T(8,128)(2,1)}, bf16[480,768]{1,0:T(8,128)(2,1)}), (bf16[8,96,768]{2,1,0:T(8,128)(2,1)}, bf16[480,768]{1,0:T(8,128)(2,1)})) %all-reduce.5.cloned.1.call-update) | async-done | bytes 1916944 | tf_op jit(solution)/shard_map/psum | solution.py:53
  205.0 5.5 %all-to-all-start.1 = ((bf16[8,96,768]{2,1,0:T(8,128)(2,1)}), bf16[8,96,768]{2,1,0:T(8,128)(2,1)}, u32[]{:S(2)}, u32[]{:S(2)}) async-start(bf16[8,96,768]{2,1,0:T(8,128)(2,1)} %get-tuple-element.20), calls=%async_computation.3 | async-start | bytes 2359296 | tf_op jit(solution)/shard_map/all_to_all | solution.py:55
  212.1 63.2 %all-reduce.1 = f32[8,672]{1,0:T(8,128)S(1)} all-reduce(f32[8,672]{1,0:T(8,128)S(1)} %concatenate.80), channel_id=7, replica_groups=mesh['dp'=4,'fsdp'=8] {'fsdp'}, use_global_device_ids=true, to_apply=%region_16.17.clone | all-reduce | flops 5376 | bytes 43008
  276.0 6.1 %psum.21 = f32[1152]{0:T(1024)S(1)} all-reduce(f32[1152]{0:T(1024)S(1)} %concatenate.81), channel_id=1, replica_groups=mesh['dp'=4,'fsdp'=8] {'dp'}, use_global_device_ids=true, to_apply=%region_19.20 | all-reduce | flops 1152 | bytes 9216 | tf_op jit(solution)/shard_map/psum | solution.py:199
  284.3 2.7 add_convert_fusion.1
  289.9 1.5 convert_element_type.125
  292.5 2.3 concatenate.84
  301.4 51.2 %reduce-scatter.3.cloned.1.call-done = bf16[128,768]{1,0:T(8,128)(2,1)} async-done(((bf16[1024,768]{1,0:T(8,128)(2,1)}), bf16[128,768]{1,0:T(8,128)(2,1)}) %reduce-scatter.3.cloned.1.call-update) | async-done | bytes 196624 | tf_op jit(solution)/shard_map/reduce_scatter | solution.py:45
  352.6 2.0 fusion.56
  (209 shorter events, 41.1 us)
Async XLA Ops:
  7.2 131.1 %copy-start = (bf16[384,768]{1,0:T(8,128)(2,1)S(1)}, bf16[384,768]{1,0:T(8,128)(2,1)}, u32[]{:S(2)}) copy-start(bf16[384,768]{1,0:T(8,128)(2,1)} %param.25) | copy-start | bytes 1769476
  7.2 90.6 %all-gather.6.cloned.1.call-start = ((), (), s32[]{:S(2)}) async-start(), calls=%async_computation.6 | async-start | bytes 1769472 | tf_op jit(solution)/shard_map/all_gather | solution.py:41
  7.2 102.6 %collective-permute-start = (bf16[96,768]{1,0:T(8,128)(2,1)}, bf16[96,768]{1,0:T(8,128)(2,1)}, u32[]{:S(2)}, u32[]{:S(2)}) collective-permute-start(bf16[96,768]{1,0:T(8,128)(2,1)} %param.21), channel_id=1, source_target_pairs={{0,1},{1,2},{2,3},{3,4},{4,5},{5,6},{6,7},{7,0},{8,9},{9,10},{10,1... | collective-permute-start | bytes 442376 | tf_op jit(solution)/shard_map/ppermute | solution.py:109
  10.3 99.5 %collective-permute-start.1 = (bf16[96,768]{1,0:T(8,128)(2,1)}, bf16[96,768]{1,0:T(8,128)(2,1)}, u32[]{:S(2)}, u32[]{:S(2)}) collective-permute-start(bf16[96,768]{1,0:T(8,128)(2,1)} %param.21), channel_id=1, source_target_pairs={{0,7},{1,0},{2,1},{3,2},{4,3},{5,4},{6,5},{7,6},{8,15},{9,8},{10,9... | collective-permute-start | bytes 442376 | tf_op jit(solution)/shard_map/ppermute | solution.py:110
  13.4 3.1 copy-start.11
  21.5 5.9 %copy-start.30 = (u32[32]{0:T(128)S(1)}, u32[32]{0:T(128)}, u32[]{:S(2)}) copy-start(u32[32]{0:T(128)} %constant.79) | copy-start | bytes 388
  21.5 7.1 %copy-start.33 = (bf16[288]{0:T(512)(128)(2,1)S(1)}, bf16[288]{0:T(512)(128)(2,1)}, u32[]{:S(2)}) copy-start(bf16[288]{0:T(512)(128)(2,1)} %param.20) | copy-start | bytes 1732
  21.5 7.1 %copy-start.36 = (bf16[96]{0:T(256)(128)(2,1)S(1)}, bf16[96]{0:T(256)(128)(2,1)}, u32[]{:S(2)}) copy-start(bf16[96]{0:T(256)(128)(2,1)} %param.15) | copy-start | bytes 580
  21.5 7.1 %copy-start.37 = (bf16[96]{0:T(256)(128)(2,1)S(1)}, bf16[96]{0:T(256)(128)(2,1)}, u32[]{:S(2)}) copy-start(bf16[96]{0:T(256)(128)(2,1)} %param.16) | copy-start | bytes 580
  21.5 7.1 %copy-start.38 = (bf16[96]{0:T(256)(128)(2,1)S(1)}, bf16[96]{0:T(256)(128)(2,1)}, u32[]{:S(2)}) copy-start(bf16[96]{0:T(256)(128)(2,1)} %param.17) | copy-start | bytes 580
  21.5 7.1 %copy-start.39 = (bf16[96]{0:T(256)(128)(2,1)S(1)}, bf16[96]{0:T(256)(128)(2,1)}, u32[]{:S(2)}) copy-start(bf16[96]{0:T(256)(128)(2,1)} %param.18) | copy-start | bytes 580
  21.5 7.1 %copy-start.40 = (bf16[96]{0:T(256)(128)(2,1)S(1)}, bf16[96]{0:T(256)(128)(2,1)}, u32[]{:S(2)}) copy-start(bf16[96]{0:T(256)(128)(2,1)} %param.22) | copy-start | bytes 580
  21.5 7.1 %copy-start.41 = (bf16[96]{0:T(256)(128)(2,1)S(1)}, bf16[96]{0:T(256)(128)(2,1)}, u32[]{:S(2)}) copy-start(bf16[96]{0:T(256)(128)(2,1)} %param.26) | copy-start | bytes 580
  21.6 73.3 %copy-start.32 = (bf16[384]{0:T(512)(128)(2,1)S(1)}, bf16[384]{0:T(512)(128)(2,1)}, u32[]{:S(2)}) copy-start(bf16[384]{0:T(512)(128)(2,1)} %param.24) | copy-start | bytes 2308
  22.3 78.1 %all-to-all-start = ((bf16[8,96,768]{2,1,0:T(8,128)(2,1)}), bf16[8,96,768]{2,1,0:T(8,128)(2,1)}, u32[]{:S(2)}, u32[]{:S(2)}) async-start(bf16[8,96,768]{2,1,0:T(8,128)(2,1)} %fusion.81), calls=%async_computation | async-start | bytes 2359296 | tf_op jit(solution)/shard_map/all_to_all | solution.py:49
  26.5 90.1 %all-gather.8.cloned.1.call-start = ((), (), s32[]{:S(2)}) async-start(), calls=%async_computation.7 | async-start | bytes 1769472 | tf_op jit(solution)/shard_map/all_gather | solution.py:41
  27.3 177.7 %all-reduce.5.cloned.1.call-start = ((), (), s32[]{:S(2)}) async-start(), calls=%async_computation.8 | async-start | bytes 3833856 | tf_op jit(solution)/shard_map/psum | solution.py:53
  94.6 5.8 %copy-start.24 = (f32[768]{0:T(1024)}, f32[768]{0:T(1024)S(1)}, u32[]{:S(2)}) copy-start(f32[768]{0:T(1024)S(1)} %add.154) | copy-start | bytes 9220
  94.7 5.7 %copy-start.26 = (f32[768]{0:T(1024)}, f32[768]{0:T(1024)S(1)}, u32[]{:S(2)}) copy-start(f32[768]{0:T(1024)S(1)} %mul.430) | copy-start | bytes 9220
  95.5 4.9 %copy-start.28 = (pred[128]{0:T(512)(128)(4,1)}, pred[128]{0:T(512)(128)(4,1)S(1)}, u32[]{:S(2)}) copy-start(pred[128]{0:T(512)(128)(4,1)S(1)} %compare_and_fusion) | copy-start | bytes 388
  105.9 3.3 copy-start.4
  118.8 6.5 %copy-start.5 = (f32[2,1024,1024]{1,2,0:T(8,128)S(1)}, f32[2,1024,1024]{1,2,0:T(8,128)}, u32[]{:S(2)}) copy-start(f32[2,1024,1024]{1,2,0:T(8,128)} %copy-done.4) | copy-start | bytes 25165828
  125.3 3.3 copy-start.18
  131.0 2.5 copy-start.19
  157.9 142.4 %reduce-scatter.5.cloned.1.call-start = ((), (), s32[]{:S(2)}) async-start(), calls=%async_computation.5 | async-start | bytes 1769472 | tf_op jit(solution)/shard_map/reduce_scatter | solution.py:45
  158.4 52.1 %copy-start.22 = (f32[8,96]{1,0:T(8,128)S(1)}, f32[8,96]{1,0:T(8,128)}, u32[]{:S(2)}) copy-start(f32[8,96]{1,0:T(8,128)} %get-tuple-element.100) | copy-start | bytes 9220
  158.4 52.2 %copy-start.21 = (f32[8,96]{1,0:T(8,128)S(1)}, f32[8,96]{1,0:T(8,128)}, u32[]{:S(2)}) copy-start(f32[8,96]{1,0:T(8,128)} %get-tuple-element.101) | copy-start | bytes 9220
  158.5 52.3 %copy-start.6 = (bf16[1,128,768]{2,1,0:T(8,128)(2,1)S(1)}, bf16[1,128,768]{2,1,0:T(8,128)(2,1)}, u32[]{:S(2)}) copy-start(bf16[1,128,768]{2,1,0:T(8,128)(2,1)} %param.14) | copy-start | bytes 589828
  205.0 84.9 %all-to-all-start.1 = ((bf16[8,96,768]{2,1,0:T(8,128)(2,1)}), bf16[8,96,768]{2,1,0:T(8,128)(2,1)}, u32[]{:S(2)}, u32[]{:S(2)}) async-start(bf16[8,96,768]{2,1,0:T(8,128)(2,1)} %get-tuple-element.20), calls=%async_computation.3 | async-start | bytes 2359296 | tf_op jit(solution)/shard_map/all_to_all | solution.py:55
  210.5 142.1 %reduce-scatter.3.cloned.1.call-start = ((), (), s32[]{:S(2)}) async-start(), calls=%async_computation.4 | async-start | bytes 1769472 | tf_op jit(solution)/shard_map/reduce_scatter | solution.py:45
  294.9 57.7 %copy-start.10 = (bf16[1,128,768]{2,1,0:T(8,128)(2,1)S(1)}, bf16[1,128,768]{2,1,0:T(8,128)(2,1)}, u32[]{:S(2)}) copy-start(bf16[1,128,768]{2,1,0:T(8,128)(2,1)} %param.27) | copy-start | bytes 589828
  296.9 57.7 %copy-start.42 = (f32[96]{0:T(128)S(1)}, f32[96]{0:T(128)}, u32[]{:S(2)}) copy-start(f32[96]{0:T(128)} %get-tuple-element.175) | copy-start | bytes 1156
  (20 other events, 28.9 us)
Sparse Core Ops, SparseCore 0:
  13.5 57.5 all-gather.5
  73.3 43.2 all-gather.7
  158.0 46.9 all-reduce.4
  208.3 76.4 reduce-scatter.4
  288.0 64.5 reduce-scatter.2
where the time goes:
time: 363 us; the launch traced here: 362 us
  blocking collectives  134 us (37%)
  waiting for transfers between devices  106 us (29%)
  matrix products  39.7 us (11%)
  local copies, waits for them, and re-layouts  28.3 us (8%)
  other arithmetic  22.5 us (6%)
  starting transfers between devices  16.1 us (4%)
  between operations  15.3 us (4%)
    unnamed x2, blocking collectives  128 us
    reduce_scatter x2, waiting for transfers between devices, scatter_rows(): return lax.psum_scatter(a, 'fsdp', scatter_dimension=0, tiled=True)  51.2 us
    psum x1, waiting for transfers between devices, return_grads(): summed = lax.psum(blocks, 'dp')  46.5 us
    dot_general x12, matrix products, dot(): lax.dot_general(a, b, ((dims[0], dims[1]), ((), ())), preferred_element_t...  23.6 us
    unnamed x110, local copies, waits for them, and re-layouts  10.9 us
  transfers between devices with their start and end apart: 9, of which 3 were waited for; matrix products, arithmetic and copies ran while one was open for 12% of the time, Pallas kernels for 0%

commit v1 on v0

--- a/solution.py
+++ b/solution.py
@@ -50,7 +50,9 @@
 
 
 def return_grads(blocks, own):
-    summed = lax.psum(blocks, "dp")
+    summed = blocks
+    for hop in (1, 2):
+        summed = summed + lax.ppermute(summed, "dp", [(dev, dev ^ hop) for dev in range(4)])
     own = lax.psum(own, "dp")
     return (lax.all_to_all(summed, "fsdp", 0, 0, tiled=True), own)
 

time: 363 us -> 344 us (0.948)
  blocking collectives: 134 us -> 115 us
  waiting for transfers between devices: 106 us -> 92.8 us
  local copies, waits for them, and re-layouts: 28.3 us -> 33.8 us
  other arithmetic: 22.5 us -> 27.7 us
    psum x1, waiting for transfers between devices: 46.5 us -> 0.02 us  [return_grads(): own = lax.psum(own, 'dp')]
    ppermute x0 -> x2, waiting for transfers between devices: none -> 31.4 us  [return_grads(): lax.ppermute(summed, 'dp', [(dev, dev ^ hop) for dev in range(4)])]
    unnamed x2, blocking collectives: 128 us -> 110 us
    reshape x4, local copies, waits for them, and re-layouts: 0.28 us -> 5.4 us  [body(): v.reshape(F, W)]
    unnamed x110 -> x134, local copies, waits for them, and re-layouts: 10.9 us -> 5.81 us
  transfers between devices with their start and end apart: 9 -> 11, of which waited for: 3 -> 3; matrix products, arithmetic and copies ran while one was open for 12% -> 19% of each run, Pallas kernels for 0% -> 0%
where the time goes in v1:
time: 344 us; the launch traced here: 343 us
  blocking collectives  115 us (33%)
  waiting for transfers between devices  92.8 us (27%)
  matrix products  41.3 us (12%)
  local copies, waits for them, and re-layouts  33.8 us (10%)
  other arithmetic  27.7 us (8%)
  starting transfers between devices  16.7 us (5%)
  between operations  15.4 us (4%)
    unnamed x2, blocking collectives  110 us
    reduce_scatter x2, waiting for transfers between devices, scatter_rows(): return lax.psum_scatter(a, 'fsdp', scatter_dimension=0, tiled=True)  54 us
    ppermute x2, waiting for transfers between devices, return_grads(): lax.ppermute(summed, 'dp', [(dev, dev ^ hop) for dev in range(4)])  31.4 us
    dot_general x12, matrix products, dot(): lax.dot_general(a, b, ((dims[0], dims[1]), ((), ())), preferred_element_t...  25.2 us
  transfers between devices with their start and end apart: 11, of which 3 were waited for; matrix products, arithmetic and copies ran while one was open for 19% of the time, Pallas kernels for 0%

profile of v1, /device:TPU:0, one launch (start us, length us, event | category | flops | bytes accessed | tf_op | source)
XLA Modules:
  0.0 343.1 jit_solution(17634597714265639272)
XLA Ops:
  7.2 3.0 collective-permute-start
  10.3 3.1 collective-permute-start.1
  13.4 1.6 reshape.208
  22.3 4.3 %all-to-all-start = ((bf16[8,96,768]{2,1,0:T(8,128)(2,1)}), bf16[8,96,768]{2,1,0:T(8,128)(2,1)}, u32[]{:S(2)}, u32[]{:S(2)}) async-start(bf16[8,96,768]{2,1,0:T(8,128)(2,1)} %fusion.81), calls=%async_computation | async-start | bytes 2359296 | tf_op jit(solution)/shard_map/all_to_all | solution.py:49
  29.0 64.7 %all-reduce = bf16[6912]{0:T(1024)(128)(2,1)S(1)} all-reduce(bf16[6912]{0:T(1024)(128)(2,1)S(1)} %dynamic-update-slice), channel_id=3, replica_groups=mesh['dp'=4,'fsdp'=8] {'fsdp'}, use_global_device_ids=true, to_apply=%add | all-reduce | flops 6912 | bytes 27648
  97.9 1.8 convert_reduce_fusion
  100.4 2.2 convolution_add_fusion.1
  104.2 1.7 select_reduce_fusion
  105.9 1.7 exponential_reduce_fusion
  107.6 1.5 copy-done.4
  109.8 6.7 %all-gather.8.cloned.1.call-done = bf16[1,1024,768]{2,1,0:T(8,128)(2,1)} async-done(((bf16[1,128,768]{2,1,0:T(8,128)(2,1)}), bf16[1,1024,768]{2,1,0:T(8,128)(2,1)}) %all-gather.8.cloned.1.call-update) | async-done | bytes 1572880 | tf_op jit(solution)/shard_map/all_gather | solution.py:41
  116.5 2.2 fusion.36
  118.7 5.8 %fusion.41 = (f32[1024,2]{0,1:T(2,128)S(1)}, bf16[2,64,1024]{2,1,0:T(8,128)(2,1)S(1)}) fusion(bf16[128,1024]{1,0:T(8,128)(2,1)S(1)} %fusion.36, bf16[1024,2,64]{0,2,1:T(8,128)(2,1)S(1)} %bitcast.331, f32[2,1024,1024]{1,2,0:T(8,128)} %copy-done.4, f32[2,1024]{1,0:T(2,128)S(1)} %copy-done.33, pred[1024,1024]{0,1:T(8,128)(4,1)S(1)} %iota_compare_fusion), kind=kOutput, calls=%fused_computation.73 | convolution fusion | flops 275249152 | bytes 10240000 | tf_op jit(solution)/shard_map/hqk,khd->qhd/dot_general | solution.py:149
  124.5 3.3 multiply_convert_fusion
  128.8 1.4 convolution_bitcast_fusion
  130.2 3.1 fusion.83
  136.1 2.7 multiply_convert_fusion.1
  138.8 1.9 convert_reduce_fusion.2
  140.8 4.0 %fusion.42 = f32[1024,768]{1,0:T(8,128)} fusion(bf16[1024,384]{1,0:T(8,128)(2,1)S(1)} %get-tuple-element.121, bf16[768,768]{1,0:T(8,128)(2,1)} %bitcast.11), kind=kOutput, calls=%fused_computation.74 | convolution fusion | flops 603979776 | bytes 4521984 | tf_op jit(solution)/shard_map/dot_general | solution.py:32
  151.9 5.3 %fusion.100 = (f32[768]{0:T(1024)}, f32[768]{0:T(1024)}, bf16[1024,768]{1,0:T(8,128)(2,1)}, f32[768]{0:T(1024)}, f32[768]{0:T(1024)}, /*index=5*/bf16[768,1024]{0,1:T(8,128)(2,1)}) fusion(f32[1024,768]{1,0:T(8,128)S(1)} %copy-done.7, f32[1024]{0:T(1024)S(1)} %add_rsqrt_fusion, f32[1024]{0:T(1024)S(1)} %broadcast_multiply_fusion.1, ...), kind=kOutput, calls=%fused_computation.217 | convolution fusion | flops 616559616 | bytes 9270272 | tf_op jit(solution)/shard_map/dot_general | solution.py:32
  157.3 3.0 copy.54
  166.3 2.7 add_convert_fusion.1
  169.0 1.6 fusion.95
  170.6 1.5 collective-permute-start.3
  172.0 31.4 %collective-permute-done.3 = bf16[8,96,768]{2,1,0:T(8,128)(2,1)S(1)} collective-permute-done((bf16[8,96,768]{2,1,0:T(8,128)(2,1)S(1)}, bf16[8,96,768]{2,1,0:T(8,128)(2,1)S(1)}, u32[]{:S(2)}, u32[]{:S(2)}) %collective-permute-start.3) | collective-permute-done | bytes 1179680 | tf_op jit(solution)/shard_map/ppermute | solution.py:55
  204.7 4.6 %all-to-all-start.1 = ((bf16[8,96,768]{2,1,0:T(8,128)(2,1)}), bf16[8,96,768]{2,1,0:T(8,128)(2,1)S(1)}, u32[]{:S(2)}, u32[]{:S(2)}) async-start(bf16[8,96,768]{2,1,0:T(8,128)(2,1)} %add.193), calls=%async_computation.3 | async-start | bytes 2359296 | tf_op jit(solution)/shard_map/all_to_all | solution.py:57
  219.0 45.1 %all-reduce.1 = f32[8,672]{1,0:T(8,128)S(1)} all-reduce(f32[8,672]{1,0:T(8,128)S(1)} %concatenate.80), channel_id=7, replica_groups=mesh['dp'=4,'fsdp'=8] {'fsdp'}, use_global_device_ids=true, to_apply=%region_16.17.clone | all-reduce | flops 5376 | bytes 43008
  265.5 5.7 %psum.14 = f32[1152]{0:T(1024)S(1)} all-reduce(f32[1152]{0:T(1024)S(1)} %concatenate.81), channel_id=1, replica_groups=mesh['dp'=4,'fsdp'=8] {'dp'}, use_global_device_ids=true, to_apply=%region_19.20 | all-reduce | flops 1152 | bytes 9216 | tf_op jit(solution)/shard_map/psum | solution.py:201
  273.0 2.2 slice.478
  275.2 1.6 slice.467
  278.1 54.0 %reduce-scatter.3.cloned.1.call-done = bf16[128,768]{1,0:T(8,128)(2,1)} async-done(((bf16[1024,768]{1,0:T(8,128)(2,1)}), bf16[128,768]{1,0:T(8,128)(2,1)}) %reduce-scatter.3.cloned.1.call-update) | async-done | bytes 196624 | tf_op jit(solution)/shard_map/reduce_scatter | solution.py:45
  332.1 2.0 fusion.56
  (239 shorter events, 50.3 us)
Async XLA Ops:
  7.2 131.6 %copy-start = (bf16[384,768]{1,0:T(8,128)(2,1)S(1)}, bf16[384,768]{1,0:T(8,128)(2,1)}, u32[]{:S(2)}) copy-start(bf16[384,768]{1,0:T(8,128)(2,1)} %param.25) | copy-start | bytes 1769476
  7.2 90.7 %all-gather.6.cloned.1.call-start = ((), (), s32[]{:S(2)}) async-start(), calls=%async_computation.7 | async-start | bytes 1769472 | tf_op jit(solution)/shard_map/all_gather | solution.py:41
  7.2 102.5 %collective-permute-start = (bf16[96,768]{1,0:T(8,128)(2,1)}, bf16[96,768]{1,0:T(8,128)(2,1)}, u32[]{:S(2)}, u32[]{:S(2)}) collective-permute-start(bf16[96,768]{1,0:T(8,128)(2,1)} %param.21), channel_id=1, source_target_pairs={{0,1},{1,2},{2,3},{3,4},{4,5},{5,6},{6,7},{7,0},{8,9},{9,10},{10,1... | collective-permute-start | bytes 442376 | tf_op jit(solution)/shard_map/ppermute | solution.py:111
  10.3 99.5 %collective-permute-start.1 = (bf16[96,768]{1,0:T(8,128)(2,1)}, bf16[96,768]{1,0:T(8,128)(2,1)}, u32[]{:S(2)}, u32[]{:S(2)}) collective-permute-start(bf16[96,768]{1,0:T(8,128)(2,1)} %param.21), channel_id=1, source_target_pairs={{0,7},{1,0},{2,1},{3,2},{4,3},{5,4},{6,5},{7,6},{8,15},{9,8},{10,9... | collective-permute-start | bytes 442376 | tf_op jit(solution)/shard_map/ppermute | solution.py:112
  21.5 5.9 %copy-start.43 = (u32[32]{0:T(128)S(1)}, u32[32]{0:T(128)}, u32[]{:S(2)}) copy-start(u32[32]{0:T(128)} %constant.79) | copy-start | bytes 388
  21.5 7.1 %copy-start.46 = (bf16[288]{0:T(512)(128)(2,1)S(1)}, bf16[288]{0:T(512)(128)(2,1)}, u32[]{:S(2)}) copy-start(bf16[288]{0:T(512)(128)(2,1)} %param.20) | copy-start | bytes 1732
  21.5 7.1 %copy-start.48 = (bf16[96]{0:T(256)(128)(2,1)S(1)}, bf16[96]{0:T(256)(128)(2,1)}, u32[]{:S(2)}) copy-start(bf16[96]{0:T(256)(128)(2,1)} %param.15) | copy-start | bytes 580
  21.5 7.1 %copy-start.49 = (bf16[96]{0:T(256)(128)(2,1)S(1)}, bf16[96]{0:T(256)(128)(2,1)}, u32[]{:S(2)}) copy-start(bf16[96]{0:T(256)(128)(2,1)} %param.16) | copy-start | bytes 580
  21.5 7.1 %copy-start.50 = (bf16[96]{0:T(256)(128)(2,1)S(1)}, bf16[96]{0:T(256)(128)(2,1)}, u32[]{:S(2)}) copy-start(bf16[96]{0:T(256)(128)(2,1)} %param.17) | copy-start | bytes 580
  21.5 7.1 %copy-start.51 = (bf16[96]{0:T(256)(128)(2,1)S(1)}, bf16[96]{0:T(256)(128)(2,1)}, u32[]{:S(2)}) copy-start(bf16[96]{0:T(256)(128)(2,1)} %param.18) | copy-start | bytes 580
  21.5 7.1 %copy-start.52 = (bf16[96]{0:T(256)(128)(2,1)S(1)}, bf16[96]{0:T(256)(128)(2,1)}, u32[]{:S(2)}) copy-start(bf16[96]{0:T(256)(128)(2,1)} %param.22) | copy-start | bytes 580
  21.5 7.1 %copy-start.53 = (bf16[96]{0:T(256)(128)(2,1)S(1)}, bf16[96]{0:T(256)(128)(2,1)}, u32[]{:S(2)}) copy-start(bf16[96]{0:T(256)(128)(2,1)} %param.26) | copy-start | bytes 580
  21.6 73.3 %copy-start.45 = (bf16[384]{0:T(512)(128)(2,1)S(1)}, bf16[384]{0:T(512)(128)(2,1)}, u32[]{:S(2)}) copy-start(bf16[384]{0:T(512)(128)(2,1)} %param.24) | copy-start | bytes 2308
  22.3 78.1 %all-to-all-start = ((bf16[8,96,768]{2,1,0:T(8,128)(2,1)}), bf16[8,96,768]{2,1,0:T(8,128)(2,1)}, u32[]{:S(2)}, u32[]{:S(2)}) async-start(bf16[8,96,768]{2,1,0:T(8,128)(2,1)} %fusion.81), calls=%async_computation | async-start | bytes 2359296 | tf_op jit(solution)/shard_map/all_to_all | solution.py:49
  26.5 89.9 %all-gather.8.cloned.1.call-start = ((), (), s32[]{:S(2)}) async-start(), calls=%async_computation.8 | async-start | bytes 1769472 | tf_op jit(solution)/shard_map/all_gather | solution.py:41
  27.3 245.7 %all-reduce.4.cloned.1.call-start = ((), (), s32[]{:S(2)}) async-start(), calls=%async_computation.6 | async-start | bytes 1474560 | tf_op jit(solution)/shard_map/psum | solution.py:56
  94.7 5.7 %copy-start.36 = (f32[768]{0:T(1024)}, f32[768]{0:T(1024)S(1)}, u32[]{:S(2)}) copy-start(f32[768]{0:T(1024)S(1)} %add.158) | copy-start | bytes 9220
  94.7 5.7 %copy-start.38 = (f32[768]{0:T(1024)}, f32[768]{0:T(1024)S(1)}, u32[]{:S(2)}) copy-start(f32[768]{0:T(1024)S(1)} %mul.430) | copy-start | bytes 9220
  118.7 5.8 %copy-start.5 = (f32[2,1024,1024]{1,2,0:T(8,128)S(1)}, f32[2,1024,1024]{1,2,0:T(8,128)}, u32[]{:S(2)}) copy-start(f32[2,1024,1024]{1,2,0:T(8,128)} %copy-done.4) | copy-start | bytes 25165828
  147.1 129.8 %reduce-scatter.5.cloned.1.call-start = ((), (), s32[]{:S(2)}) async-start(), calls=%async_computation.5 | async-start | bytes 1769472 | tf_op jit(solution)/shard_map/reduce_scatter | solution.py:45
  157.2 174.9 %reduce-scatter.3.cloned.1.call-start = ((), (), s32[]{:S(2)}) async-start(), calls=%async_computation.4 | async-start | bytes 1769472 | tf_op jit(solution)/shard_map/reduce_scatter | solution.py:45
  165.3 3.7 %collective-permute-start.2 = (bf16[8,96,768]{2,1,0:T(8,128)(2,1)}, bf16[8,96,768]{2,1,0:T(8,128)(2,1)}, u32[]{:S(2)}, u32[]{:S(2)}) collective-permute-start(bf16[8,96,768]{2,1,0:T(8,128)(2,1)} %pad_maximum_fusion.1), channel_id=1, source_target_pairs={{0,8},{8,0},{16,24},{24,16},{1,9},{9,1},{17,25},{25,17},{2,10},{10... | collective-permute-start | bytes 3538952 | tf_op jit(solution)/shard_map/ppermute | solution.py:55
  170.6 32.8 %collective-permute-start.3 = (bf16[8,96,768]{2,1,0:T(8,128)(2,1)S(1)}, bf16[8,96,768]{2,1,0:T(8,128)(2,1)S(1)}, u32[]{:S(2)}, u32[]{:S(2)}) collective-permute-start(bf16[8,96,768]{2,1,0:T(8,128)(2,1)S(1)} %fusion.95), channel_id=1, source_target_pairs={{0,16},{8,24},{16,0},{24,8},{1,17},{9,25},{17,1},{25,9},{2,18},{10... | collective-permute-start | bytes 3538952 | tf_op jit(solution)/shard_map/ppermute | solution.py:55
  204.7 5.3 %copy-start.6 = (bf16[1,128,768]{2,1,0:T(8,128)(2,1)S(1)}, bf16[1,128,768]{2,1,0:T(8,128)(2,1)}, u32[]{:S(2)}) copy-start(bf16[1,128,768]{2,1,0:T(8,128)(2,1)} %param.14) | copy-start | bytes 589828
  204.7 13.1 %copy-start.3 = (bf16[1,1024,768]{2,1,0:T(8,128)(2,1)S(1)}, bf16[1,1024,768]{2,1,0:T(8,128)(2,1)}, u32[]{:S(2)}) copy-start(bf16[1,1024,768]{2,1,0:T(8,128)(2,1)} %all-gather.8.cloned.1.call-done) | copy-start | bytes 4718596
  204.7 129.3 %all-to-all-start.1 = ((bf16[8,96,768]{2,1,0:T(8,128)(2,1)}), bf16[8,96,768]{2,1,0:T(8,128)(2,1)S(1)}, u32[]{:S(2)}, u32[]{:S(2)}) async-start(bf16[8,96,768]{2,1,0:T(8,128)(2,1)} %add.193), calls=%async_computation.3 | async-start | bytes 2359296 | tf_op jit(solution)/shard_map/all_to_all | solution.py:57
  212.4 5.8 %copy-start.28 = (f32[8,288]{1,0:T(8,128)S(1)}, f32[8,288]{1,0:T(8,128)}, u32[]{:S(2)}) copy-start(f32[8,288]{1,0:T(8,128)} %reshape.220) | copy-start | bytes 27652
  218.1 58.8 %copy-start.35 = (f32[128]{0:T(128)S(1)}, f32[128]{0:T(128)}, u32[]{:S(2)}) copy-start(f32[128]{0:T(128)} %copy-done.34) | copy-start | bytes 1540
  218.1 58.8 %copy-start.42 = (f32[128]{0:T(128)S(1)}, f32[128]{0:T(128)}, u32[]{:S(2)}) copy-start(f32[128]{0:T(128)} %add_rsqrt_fusion.1) | copy-start | bytes 1540
  273.0 63.1 %copy-start.54 = (f32[96]{0:T(128)}, f32[96]{0:T(128)S(1)}, u32[]{:S(2)}) copy-start(f32[96]{0:T(128)S(1)} %get-tuple-element.173) | copy-start | bytes 1156
  273.0 59.1 %copy-start.16 = (bf16[1,128,768]{2,1,0:T(8,128)(2,1)S(1)}, bf16[1,128,768]{2,1,0:T(8,128)(2,1)}, u32[]{:S(2)}) copy-start(bf16[1,128,768]{2,1,0:T(8,128)(2,1)} %param.27) | copy-start | bytes 589828
  273.0 59.1 %copy-start.30 = (f32[768]{0:T(1024)S(1)}, f32[768]{0:T(1024)}, u32[]{:S(2)}) copy-start(f32[768]{0:T(1024)} %add.181) | copy-start | bytes 9220
  (34 other events, 84.4 us)
Sparse Core Ops, SparseCore 0:
  13.5 57.5 all-gather.5
  73.3 43.1 all-gather.7
  147.2 35.7 all-reduce.3
  186.3 77.8 reduce-scatter.4
  267.4 64.5 reduce-scatter.2
